TPU v7x, 1024 devices: a whole 4x4x32 slice. The times are simulated.
1024 devices in a mesh: dp: 128 (over y_lo, z, core), tensor: 4 (over x), group: 2 (over y_hi).
Axes of the slice: x: 4, y: 4 (y_hi: 2, y_lo: 2; y = y_hi * 2 + y_lo), z: 32, core: 2. Of those that a mesh axis runs over, the one named last changes fastest.
Arguments:
- tokens: bfloat16 [32768, 5120], P(('dp', 'group')), may hold values from -6 to 6
- cotangent: bfloat16 [32768, 1024], P(('dp', 'group'), 'tensor'), may hold values from -0.032958984 to 0.032958984
- counts: int32 [256], replicated, may hold values from 32 to 128, as said below
- old_offsets: int32 [8, 129], replicated, may hold values from 0 to 655360, as said below
- old_master: float32 [8, 128, 6400], P(('tensor', 'group'), 'dp'), may hold values from -0.078125 to 0.078125
- old_moment: float32 [8, 128, 6400], P(('tensor', 'group'), 'dp'), may hold values from -3 to 3
- old_variance: float32 [8, 128, 6400], P(('tensor', 'group'), 'dp'), may hold values from 0.001 to 1
- old_grad: float32 [8, 128, 6400], P(('tensor', 'group'), 'dp'), may hold values from -6 to 6
Outputs:
- activated: bfloat16 [32768, 1024], P(('dp', 'group'), 'tensor')
- new_master: float32 [5120, 1024], P(('dp', 'group'), 'tensor')
- new_moment: float32 [5120, 1024], P(('dp', 'group'), 'tensor')
- new_variance: float32 [5120, 1024], P(('dp', 'group'), 'tensor')
Inputs may be any that keep to these rules, and one draw needn't show every extreme that they name: `counts`: each new data rank has between 32 and 128 live tokens, which fill its first slots; in every draw some rank has exactly 128. `old_offsets`: each row starts at 0 and ends at 655360; entry p lies within 640 of p * 5120; in every row some entry p with 0 < p < 128 equals p * 5120 + 640.
All inputs are finite; a program needn't handle non-finite values.
Results may differ from a plain program's by a relative error of at most 0.0051.
Values may be sent and summed in bfloat16 or wider, within the bound.
A program may use at most 32 MiB of HBM per device.

v0:
```python
import jax
import jax.numpy as jnp
from jax import lax
from jax.sharding import PartitionSpec as P

KV = 1024


beta_one = 0.9
beta_two = 0.95
epsilon = 1e-08
learn_rate = 0.001
weight_decay = 0.1
first_step = 3.0
second_step = 4.0


def padded_2(cells, sides, width):
    for axis, dim in sides:
        count = lax.axis_size(axis)
        ends = count - 1
        head = lax.slice_in_dim(cells, 0, width, axis=dim)
        tail = lax.slice_in_dim(cells, cells.shape[dim] - width, cells.shape[dim], axis=dim)
        cells = jnp.concatenate(
            [
                lax.ppermute(tail, axis, [(i, (i + 1) % count) for i in range(ends)]),
                cells,
                lax.ppermute(head, axis, [((i + 1) % count, i) for i in range(ends)]),
            ],
            axis=dim,
        )
    return cells


def partner(value, axis, bit):
    mask = 2**bit
    pairs = [(source, source ^ mask) for source in range(lax.axis_size(axis))]
    return lax.ppermute(value, axis, pairs)


def adam_update(master, moment, variance, gradient, step_count):
    moment = beta_one * moment + (1.0 - beta_one) * gradient
    variance = beta_two * variance + (1.0 - beta_two) * gradient * gradient
    fix_one = 1.0 - beta_one**step_count
    fix_two = 1.0 - beta_two**step_count
    update = moment / fix_one / (jnp.sqrt(variance / fix_two) + epsilon) + weight_decay * master
    return (master - learn_rate * update, moment, variance)


def local(tokens, cotangent, counts, old_offsets, old_master, old_moment, old_variance, old_grad):
    group_size = lax.axis_size("group")
    group_index = lax.axis_index("group")
    owner_rank = lax.axis_index("dp")
    old_slab = lax.axis_index("tensor") * group_size + group_index
    master, moment, variance = adam_update(
        old_master[0, 0], old_moment[0, 0], old_variance[0, 0], old_grad[0, 0], first_step
    )
    window = master.shape[0]
    margin = window // 10
    shard_len = 8 * margin
    old_cols = KV // (lax.axis_size("tensor") * group_size)
    piece_rows = shard_len // old_cols
    tile_rows = piece_rows // 2
    bounds = lax.dynamic_slice(old_offsets, (old_slab, owner_rank), (1, 2))[0]
    position = owner_rank * shard_len - margin + jnp.arange(window, dtype=jnp.int32)
    is_live = (position >= bounds[0]) & (position < bounds[1])
    stacked = jnp.where(is_live[None, :], jnp.stack([master, moment, variance]), jnp.float32(0.0))
    padded = padded_2(stacked, (("dp", 1),), margin)
    rebuilt = padded[:, 2 * margin : 2 * margin + shard_len]
    rebuilt = rebuilt + jnp.pad(padded[:, :margin], ((0, 0), (0, shard_len - margin)))
    rebuilt = rebuilt + jnp.pad(
        padded[:, shard_len + 3 * margin :], ((0, 0), (shard_len - margin, 0))
    )
    rebuilt = rebuilt.reshape(3, piece_rows, old_cols)
    outgoing = lax.dynamic_slice_in_dim(rebuilt, (1 - group_index) * tile_rows, tile_rows, 1)
    staying = lax.dynamic_slice_in_dim(rebuilt, group_index * tile_rows, tile_rows, 1)
    incoming = partner(outgoing, "group", 0)
    low_cols = jnp.where(group_index == 0, staying, incoming)
    high_cols = jnp.where(group_index == 0, incoming, staying)
    states = jnp.concatenate([low_cols, high_cols], axis=2)
    weights = states[0].astype(jnp.bfloat16)
    preact = jnp.dot(
        tokens,
        lax.all_gather(weights, ("dp", "group"), axis=0, tiled=True),
        preferred_element_type=jnp.float32,
    )
    activated = jax.nn.silu(preact).astype(jnp.bfloat16)
    sigmoid_z = jax.nn.sigmoid(preact)
    derivative = sigmoid_z * (1.0 + preact * (1.0 - sigmoid_z))
    my_count = counts[owner_rank * group_size + group_index]
    row_live = jnp.arange(tokens.shape[0], dtype=jnp.int32) < my_count
    delta = jnp.where(
        row_live[:, None], cotangent.astype(jnp.float32) * derivative, jnp.float32(0.0)
    ).astype(jnp.bfloat16)
    contract = (((0,), (0,)), ((), ()))
    full_grad = lax.dot_general(tokens, delta, contract, preferred_element_type=jnp.float32)
    gradient = lax.psum_scatter(full_grad, ("dp", "group"), scatter_dimension=0, tiled=True)
    new_master, new_moment, new_variance = adam_update(
        states[0], states[1], states[2], gradient, second_step
    )
    return (activated, new_master, new_moment, new_variance)


def solution(mesh):
    return jax.shard_map(
        local,
        mesh=mesh,
        in_specs=(
            P(("dp", "group"), None),
            P(("dp", "group"), "tensor"),
            P(),
            P(),
            P(("tensor", "group"), "dp", None),
            P(("tensor", "group"), "dp", None),
            P(("tensor", "group"), "dp", None),
            P(("tensor", "group"), "dp", None),
        ),
        out_specs=(
            P(("dp", "group"), "tensor"),
            P(("dp", "group"), "tensor"),
            P(("dp", "group"), "tensor"),
            P(("dp", "group"), "tensor"),
        ),
        check_vma=False,
    )
```

profile of v0, /device:TPU:6, one launch (start us, length us, event | category | flops | bytes accessed | tf_op | source)
XLA Modules:
  0.0 1472.2 jit_solution(16362864644460448698)
XLA Ops:
  7.2 0.0 copy-start
  7.2 0.0 all-gather.3.cloned.1.call-start
  7.2 0.9 dynamic_slice.12
  8.1 0.6 fusion.28
  8.7 1.3 fusion.7
  10.0 1.0 bitcast_subtract_fusion
  11.0 0.1 maximum_select_fusion
  11.1 1.3 collective-permute-start.1
  12.4 3.0 collective-permute-start
  15.4 0.0 collective-permute-done.1
  15.4 0.8 collective-permute-done
  16.3 5.1 collective-permute-start.2
  21.4 2.2 collective-permute-done.2
  23.7 0.6 convert_bitcast_fusion
  24.3 0.0 all-gather.3.cloned.1.call-update
  24.3 0.0 all-reduce.5.cloned.1.call-start
  24.3 1.0 copy.25
  25.3 1.3 dynamic_slice.15
  26.6 0.6 iota_compare_fusion
  27.2 739.3 %all-gather.3.cloned.1.call-done = bf16[256,20,256]{2,1,0:T(8,128)(2,1)} async-done(((bf16[1,20,256]{2,1,0:T(8,128)(2,1)}), bf16[256,20,256]{2,1,0:T(8,128)(2,1)}) %all-gather.3.cloned.1.call-update) | async-done | bytes 2621456 | tf_op jit(solution)/shard_map/all_gather | solution.py:84
  766.5 5.2 reshape.149
  771.7 0.0 copy-done
  771.7 2.6 multiply_convert_fusion
  774.3 3.2 convolution_bitcast_fusion
  777.5 0.0 all-reduce.5.cloned.1.call-update
  777.5 1.3 dynamic-slice
  779.5 0.7 copy.29
  780.2 683.3 %all-reduce.5.cloned.1.call-done = f32[5120,256]{0,1:T(8,128)} async-done(((f32[5120,256]{0,1:T(8,128)}), f32[5120,256]{0,1:T(8,128)}) %all-reduce.5.cloned.1.call-update) | async-done | bytes 5242896
  1463.5 1.0 constant_dynamic-slice_fusion
  1464.6 0.1 copy.26
  1464.7 0.7 multiply_subtract_fusion
  (5 shorter events, 0.1 us)
Async XLA Ops:
  7.2 764.5 %copy-start = (bf16[128,5120]{1,0:T(8,128)(2,1)S(1)}, bf16[128,5120]{1,0:T(8,128)(2,1)}, u32[]{:S(2)}) copy-start(bf16[128,5120]{1,0:T(8,128)(2,1)} %param.8) | copy-start | bytes 3932164
  7.2 759.3 %all-gather.3.cloned.1.call-start = ((), (), s32[]{:S(2)}) async-start(), calls=%async_computation | async-start | bytes 3158016 | tf_op jit(solution)/shard_map/all_gather | solution.py:84
  11.1 4.3 collective-permute-start.1
  12.4 3.9 collective-permute-start
  16.3 7.4 collective-permute-start.2
  24.3 1439.2 %all-reduce.5.cloned.1.call-start = ((), (), s32[]{:S(2)}) async-start(), calls=%async_computation.1 | async-start | bytes 10485760
Sparse Core Ops, SparseCore 0:
  24.4 742.0 all-gather.2
  777.7 685.8 all-reduce.4
where the time goes:
time: 1470 us
  waiting for transfers between devices  1430 us (97%)
  between operations  14.8 us (1%)
    all_gather x1, waiting for transfers between devices, local(): lax.all_gather(weights, ('dp', 'group'), axis=0, tiled=True)  739 us
    unnamed x3, waiting for transfers between devices  683 us
  transfers between devices with their start and end apart: 5, of which 4 were waited for; matrix products, arithmetic and copies ran while one was open for 0% of the time, Pallas kernels for 0%

commit v1 on v0

v1 whole, which is shorter than its diff:
```python
import functools

import jax
import jax.numpy as jnp
from jax import lax
from jax.experimental import pallas as pl
from jax.experimental.pallas import tpu as pltpu
from jax.sharding import PartitionSpec as P

MESH = pl.DeviceIdType.MESH
F32 = jnp.float32
BF16 = jnp.bfloat16

beta_one = 0.9
beta_two = 0.95
epsilon = 1e-08
learn_rate = 0.001
weight_decay = 0.1
first_step = 3.0
second_step = 4.0

LANES = 128
STRIDE = 4


def adam_update(master, moment, variance, gradient, step_count):
    moment = beta_one * moment + (1.0 - beta_one) * gradient
    variance = beta_two * variance + (1.0 - beta_two) * gradient * gradient
    fix_one = 1.0 - beta_one**step_count
    fix_two = 1.0 - beta_two**step_count
    update = moment / fix_one / (jnp.sqrt(variance / fix_two) + epsilon) + weight_decay * master
    return (master - learn_rate * update, moment, variance)


def kernel(
    dp_size,
    offsets,
    counts,
    tok_hbm,
    cot,
    old_master,
    old_moment,
    old_variance,
    old_grad,
    act_out,
    master_out,
    moment_out,
    variance_out,
    tok,
    tok_t,
    old,
    live_state,
    edge_out,
    edge_in,
    state,
    w,
    w_flat,
    parts,
    core_in,
    y_in,
    z_sum,
    near_in,
    plus_out,
    plus_in,
    minus_out,
    minus_in,
    tile_out,
    tile_in,
    tok_sem,
    edge_sems,
    ring_send,
    z_recv,
    near_send,
    y_send,
    y_recv,
    core_send,
    core_recv,
    part_send,
    part_recv,
    sum_send,
    sum_recv,
    window_send,
    window_recv,
    plus_sems,
    minus_sems,
    tile_sems,
):
    depth = dp_size // 4
    members = depth // STRIDE
    half = members // 2
    rows = state.shape[1]
    window_rows = old.shape[1]
    margin = (window_rows - rows) // 2
    tile = rows // 2

    dp = lax.axis_index("dp")
    group = lax.axis_index("group")
    tensor = lax.axis_index("tensor")
    core = lax.rem(dp, 2)
    z = lax.rem(lax.div(dp, 2), depth)
    y_lo = lax.div(dp, 2 * depth)
    a = lax.div(z, STRIDE)
    b = lax.rem(z, STRIDE)

    def device(dz=0, flip_lo=0, flip_group=0, flip_core=0):
        to_z = lax.rem(z + dz + depth, depth)
        to_lo = 1 - y_lo if flip_lo else y_lo
        to_core = 1 - core if flip_core else core
        to_group = 1 - group if flip_group else group
        return {"dp": (to_lo * depth + to_z) * 2 + to_core, "group": to_group}

    right = {"dp": lax.rem(dp + 1, dp_size), "group": group}
    left = {"dp": lax.rem(dp + dp_size - 1, dp_size), "group": group}
    other_core = device(flip_core=1)
    y_flips = ((1, 0), (1, 1), (0, 1))
    y_peers = [device(flip_lo=l, flip_group=g) for l, g in y_flips]

    def remote(src, dst, send_sem, recv_sem, to):
        return pltpu.make_async_remote_copy(
            src_ref=src,
            dst_ref=dst,
            send_sem=send_sem,
            recv_sem=recv_sem,
            device_id=to,
            device_id_type=MESH,
        )

    pending = []

    def send(src, dst, send_sem, recv_sem, to):
        copy = remote(src, dst, send_sem, recv_sem, to)
        copy.start()
        pending.append(copy)

    def arrived(dst, recv_sem):
        remote(dst, dst, recv_sem, recv_sem, other_core).wait_recv()

    tok_copy = pltpu.make_async_copy(tok_hbm, tok, tok_sem)
    tok_copy.start()

    barrier = pltpu.get_barrier_semaphore()
    greeted = [right, left, other_core, *y_peers]
    greeted += [device(dz=d) for d in (STRIDE, -STRIDE, 1, -1, 2, -2)]
    for peer in greeted:
        pl.semaphore_signal(barrier, inc=1, device_id=peer, device_id_type=MESH)

    for r in range(window_rows):
        lanes = slice(r * LANES, (r + 1) * LANES)
        for i, ref in enumerate((old_master, old_moment, old_variance, old_grad)):
            old[i, r : r + 1, :] = ref[0, :, lanes]
    updated = adam_update(old[0], old[1], old[2], old[3], first_step)
    shape = (window_rows, LANES)
    position = (
        dp * (rows * LANES)
        - margin * LANES
        + lax.broadcasted_iota(jnp.int32, shape, 0) * LANES
        + lax.broadcasted_iota(jnp.int32, shape, 1)
    )
    slab = tensor * 2 + group
    low, high = offsets[slab, dp], offsets[slab, dp + 1]
    is_live = (position >= low) & (position < high)
    for i in range(3):
        live_state[i] = jnp.where(is_live, updated[i], F32(0.0))
    for i in range(3):
        edge_out[0, i] = live_state[i, rows + margin : window_rows, :]
        edge_out[1, i] = live_state[i, 0:margin, :]
    pl.semaphore_wait(barrier, len(greeted))
    send(edge_out.at[0], edge_in.at[0], edge_sems.at[0], edge_sems.at[2], right)
    send(edge_out.at[1], edge_in.at[1], edge_sems.at[1], edge_sems.at[3], left)
    for i in range(3):
        state[i] = live_state[i, margin : margin + rows, :]
    arrived(edge_in.at[0], edge_sems.at[2])
    arrived(edge_in.at[1], edge_sems.at[3])
    for i in range(3):
        state[i, 0:margin, :] += edge_in[0, i]
        state[i, rows - margin : rows, :] += edge_in[1, i]

    line = w.at[group, y_lo, core]
    line[z] = state[0].astype(BF16)

    def at(k):
        return lax.rem(z + STRIDE * k + depth, depth)

    def ring(slot, step, direction):
        index = step if direction > 0 else half + step
        send(line.at[slot], line.at[slot], ring_send.at[index], z_recv.at[slot], device(dz=direction * STRIDE))

    def near(slot):
        block = lax.div(slot, STRIDE)
        far = 2 - 4 * lax.rem(block, 2)
        for i, d in enumerate((1, -1, far)):
            send(line.at[slot], line.at[slot], near_send.at[i, block], z_recv.at[slot], device(dz=d))

    def along_y(k):
        block = lax.rem(a + k + members, members)
        for d in range(1, STRIDE):
            slot = block * STRIDE + lax.rem(b + d, STRIDE)
            arrived(line.at[slot], z_recv.at[slot])
        piece = line.at[pl.ds(block * STRIDE, STRIDE)]
        for i, peer in enumerate(y_peers):
            send(piece, piece, y_send.at[i, block], y_recv.at[i, block], peer)

    ring(z, 0, 1)
    if half > 1:
        ring(z, 0, -1)
    near(z)

    tok_copy.wait()
    for i in range(tok.shape[1] // LANES):
        lanes = slice(i * LANES, (i + 1) * LANES)
        tok_t[lanes, :] = tok[:, lanes].T

    for k in range(1, half + 1):
        slot = at(-k)
        arrived(line.at[slot], z_recv.at[slot])
        if k < half:
            ring(slot, k, 1)
        near(slot)
        if k < half:
            slot = at(k)
            arrived(line.at[slot], z_recv.at[slot])
            if k < half - 1:
                ring(slot, k, -1)
            near(slot)
        along_y(1 - k)
        if k > 1:
            along_y(k - 1)
    along_y(half)

    def to_core(i, lo, g):
        src = w.at[g, lo, core]
        send(src, src, core_send.at[i], core_recv.at[i], other_core)

    def lines(i):
        l, g = ((0, 0),) [0] if i == 0 else y_flips[i - 1]
        return (1 - y_lo if l else y_lo), (1 - group if g else group)

    to_core(0, y_lo, group)
    for i in range(3):
        lo, g = lines(i + 1)
        for block in range(members):
            src = w.at[g, lo, core, pl.ds(block * STRIDE, STRIDE)]
            arrived(src, y_recv.at[i, block])
        to_core(i + 1, lo, g)
    for i in range(4):
        lo, g = lines(i)
        arrived(w.at[g, lo, 1 - core], core_recv.at[i])

    def flatten(zz, carry):
        for lo in range(2):
            start = pl.multiple_of((lo * depth + zz) * (2 * rows), 2 * rows)
            for g in range(2):
                both = jnp.concatenate([w[g, lo, 0, zz], w[g, lo, 1, zz]], axis=0)
                w_flat[pl.ds(start, 2 * rows), g * LANES : (g + 1) * LANES] = both
        return carry

    lax.fori_loop(0, depth, flatten, 0)
    preact = jnp.dot(tok[...], w_flat[...], preferred_element_type=F32)
    sigmoid_z = jax.nn.sigmoid(preact)
    act_out[...] = (preact * sigmoid_z).astype(BF16)
    derivative = sigmoid_z * (1.0 + preact * (1.0 - sigmoid_z))
    my_count = counts[dp * 2 + group]
    row_live = lax.broadcasted_iota(jnp.int32, preact.shape, 0) < my_count
    delta = jnp.where(row_live, cot[...].astype(F32) * derivative, F32(0.0)).astype(BF16)

    order = [half] + [s * k for k in range(half - 1, 0, -1) for s in (1, -1)] + [0]
    blocks = [lax.rem(a + k + members, members) for k in order]
    for block in blocks:
        for lo in range(2):
            count = STRIDE * 2 * rows
            start = pl.multiple_of((lo * depth + block * STRIDE) * (2 * rows), count)
            part = jnp.dot(tok_t[pl.ds(start, count), :], delta, preferred_element_type=F32)
            for zz in range(STRIDE):
                for c in range(2):
                    top = (zz * 2 + c) * rows
                    for g in range(2):
                        parts[c, block, g, lo, zz] = part[top : top + rows, g * LANES : (g + 1) * LANES].astype(BF16)
        send(parts.at[1 - core, block], core_in.at[block], part_send.at[block], part_recv.at[block], other_core)
    for block in blocks:
        arrived(core_in.at[block], part_recv.at[block])
        both = parts[core, block].astype(F32) + core_in[block].astype(F32)
        parts[core, block] = both.astype(BF16)
        for i, (l, g) in enumerate(y_flips):
            lo = 1 - y_lo if l else y_lo
            gg = 1 - group if g else group
            send(parts.at[core, block, gg, lo], y_in.at[i, block], sum_send.at[i, block], sum_recv.at[i, block], y_peers[i])

    def over_y(j):
        block = blocks[j]
        total = parts[core, block, group, y_lo].astype(F32)
        for i in range(3):
            arrived(y_in.at[i, block], sum_recv.at[i, block])
            total += y_in[i, block].astype(F32)
        z_sum[block] = total.astype(BF16)
        far = 2 - 4 * lax.rem(block, 2)
        for i, (d, dz) in enumerate(((1, 1), (3, -1), (2, far))):
            src = z_sum.at[block, lax.rem(b + d, STRIDE)]
            send(src, near_in.at[i, block], window_send.at[i, block], window_recv.at[i, block], device(dz=dz))

    def over_ring(j):
        block, k = blocks[j], order[j]
        total = z_sum[block, b].astype(F32)
        for i in range(3):
            arrived(near_in.at[i, block], window_recv.at[i, block])
            total += near_in[i, block].astype(F32)
        if k >= 0 and k < half:
            s = half - 1 - k
            arrived(plus_in.at[s], plus_sems.at[1, s])
            total += plus_in[s].astype(F32)
        if k <= 0 and -k < half - 1:
            s = half - 2 + k
            arrived(minus_in.at[s], minus_sems.at[1, s])
            total += minus_in[s].astype(F32)
        if k > 0:
            s = half - k
            plus_out[s] = total.astype(BF16)
            send(plus_out.at[s], plus_in.at[s], plus_sems.at[0, s], plus_sems.at[1, s], device(dz=STRIDE))
        if k < 0:
            s = half - 1 + k
            minus_out[s] = total.astype(BF16)
            send(minus_out.at[s], minus_in.at[s], minus_sems.at[0, s], minus_sems.at[1, s], device(dz=-STRIDE))
        return total

    for j in range(members + 1):
        if j < members:
            over_y(j)
        if j >= 1:
            gradient = over_ring(j - 1)

    new = adam_update(state[0], state[1], state[2], gradient, second_step)
    first = group == 0
    for i in range(3):
        state[i] = new[i]
        top, bottom = state[i, 0:tile, :], state[i, tile:rows, :]
        tile_out[i] = jnp.where(first, bottom, top)
    send(tile_out, tile_in, tile_sems.at[0], tile_sems.at[1], y_peers[2])
    arrived(tile_in, tile_sems.at[1])
    for i, ref in enumerate((master_out, moment_out, variance_out)):
        top, bottom = state[i, 0:tile, :], state[i, tile:rows, :]
        kept = jnp.where(first, top, bottom)
        ref[:, 0:LANES] = jnp.where(first, kept, tile_in[i])
        ref[:, LANES : 2 * LANES] = jnp.where(first, tile_in[i], kept)
    for copy in pending:
        copy.wait_send()


def solution(mesh):
    dp_size = mesh.shape["dp"]
    depth = dp_size // 4
    members = depth // STRIDE
    half = members // 2

    def local(tokens, cotangent, counts, old_offsets, old_master, old_moment, old_variance, old_grad):
        token_rows, width = tokens.shape
        window_rows = old_master.shape[-1] // LANES
        rows = width // dp_size
        margin = (window_rows - rows) // 2
        tile = rows // 2
        out = jax.ShapeDtypeStruct((tile, 2 * LANES), F32)
        piece = (rows, LANES)
        vmem = pl.BlockSpec(memory_space=pltpu.VMEM)
        smem = pl.BlockSpec(memory_space=pltpu.SMEM)
        dma = pltpu.SemaphoreType.DMA
        return pl.pallas_call(
            functools.partial(kernel, dp_size),
            out_shape=(jax.ShapeDtypeStruct(cotangent.shape, BF16), out, out, out),
            in_specs=[smem, smem, pl.BlockSpec(memory_space=pl.ANY)] + [vmem] * 5,
            out_specs=(vmem,) * 4,
            scratch_shapes=[
                pltpu.VMEM((token_rows, width), BF16),
                pltpu.VMEM((width, token_rows), BF16),
                pltpu.VMEM((4, window_rows, LANES), F32),
                pltpu.VMEM((3, window_rows, LANES), F32),
                pltpu.VMEM((2, 3, margin, LANES), F32),
                pltpu.VMEM((2, 3, margin, LANES), F32),
                pltpu.VMEM((3, *piece), F32),
                pltpu.VMEM((2, 2, 2, depth, *piece), BF16),
                pltpu.VMEM((width, 2 * LANES), BF16),
                pltpu.VMEM((2, members, 2, 2, STRIDE, *piece), BF16),
                pltpu.VMEM((members, 2, 2, STRIDE, *piece), BF16),
                pltpu.VMEM((3, members, STRIDE, *piece), BF16),
                pltpu.VMEM((members, STRIDE, *piece), BF16),
                pltpu.VMEM((3, members, *piece), BF16),
                pltpu.VMEM((half, *piece), BF16),
                pltpu.VMEM((half, *piece), BF16),
                pltpu.VMEM((half, *piece), BF16),
                pltpu.VMEM((half, *piece), BF16),
                pltpu.VMEM((3, tile, LANES), F32),
                pltpu.VMEM((3, tile, LANES), F32),
                dma(()),
                dma((4,)),
                dma((2 * half,)),
                dma((depth,)),
                dma((3, members)),
                dma((3, members)),
                dma((3, members)),
                dma((4,)),
                dma((4,)),
                dma((members,)),
                dma((members,)),
                dma((3, members)),
                dma((3, members)),
                dma((3, members)),
                dma((3, members)),
                dma((2, half)),
                dma((2, half)),
                dma((2,)),
            ],
            compiler_params=pltpu.CompilerParams(collective_id=0, has_side_effects=True),
        )(old_offsets, counts, tokens, cotangent, old_master, old_moment, old_variance, old_grad)

    state_spec = P(("tensor", "group"), "dp", None)
    row_spec = P(("dp", "group"), "tensor")
    return jax.shard_map(
        local,
        mesh=mesh,
        in_specs=(P(("dp", "group"), None), row_spec, P(), P(), state_spec, state_spec, state_spec, state_spec),
        out_specs=(row_spec,) * 4,
        check_vma=False,
    )
```

time: 1470 us -> 117 us (0.08)
  waiting for transfers between devices: 1430 us -> 0 us
  Pallas kernels: 0 us -> 111 us
    all_gather x1 -> x0, waiting for transfers between devices: 739 us -> none  [local(): lax.all_gather(weights, ('dp', 'group'), axis=0, tiled=True)]
    unnamed x3 -> x0, waiting for transfers between devices: 683 us -> none
    pallas_call x0 -> x1, Pallas kernels: none -> 111 us  [local(): pl.pallas_call(functools.partial(kernel, dp_size), out_shape=(jax.ShapeDt...]
  transfers between devices with their start and end apart: 5 -> 0, of which waited for: 4 -> 0; matrix products, arithmetic and copies ran while one was open for 0% -> 0% of each run, Pallas kernels for 0% -> 0%
where the time goes in v1:
time: 117 us
  Pallas kernels  111 us (95%)
  local copies, waits for them, and re-layouts  5.51 us (5%)
    pallas_call x1, Pallas kernels, local(): pl.pallas_call(functools.partial(kernel, dp_size), out_shape=(jax.ShapeDt...  111 us
    unnamed x4, local copies, waits for them, and re-layouts  5.51 us

profile of v1, /device:TPU:6, one launch (start us, length us, event | category | flops | bytes accessed | tf_op | source)
XLA Modules:
  0.0 116.7 jit_solution(4066962722115590851)
XLA Ops:
  0.6 110.5 %shard_map.111 = (bf16[128,256]{1,0:T(8,128)(2,1)}, f32[20,256]{1,0:T(8,128)}, f32[20,256]{1,0:T(8,128)}, f32[20,256]{1,0:T(8,128)}) custom-call(s32[8,129]{1,0:T(8,128)} %offsets.1, s32[256]{0:T(256)} %counts.1, bf16[128,5120]{1,0:T(8,128)(2,1)} %tok_hbm.1, bf16[128,256]{1,0:T(8,128)(2,1)} %cot.1, f32[1,1,6400]{2,1,0:T(1,128)} %old_master.1, ...), custom_call_target="tpu_custom_call" | custom-call | tf_op jit(solution)/shard_map/pallas_call | solution.py:364
  111.2 1.5 %copy.16 = bf16[128,256]{1,0:T(8,128)(2,1)} copy(bf16[128,256]{1,0:T(8,128)(2,1)} %get-tuple-element.8) | data formatting | bytes 131072
  112.6 1.3 %copy.17 = f32[20,256]{1,0:T(8,128)} copy(f32[20,256]{1,0:T(8,128)} %get-tuple-element.9) | data formatting | bytes 40960
  114.0 1.3 %copy.18 = f32[20,256]{1,0:T(8,128)} copy(f32[20,256]{1,0:T(8,128)} %get-tuple-element.10) | data formatting | bytes 40960
  115.3 1.3 %copy.19 = f32[20,256]{1,0:T(8,128)} copy(f32[20,256]{1,0:T(8,128)} %get-tuple-element.11) | data formatting | bytes 40960

commit v2 on v1

--- a/solution.py
+++ b/solution.py
@@ -20,6 +20,7 @@
 second_step = 4.0
 
 LANES = 128
+IN_FLIGHT = 2
 STRIDE = 4
 
 
@@ -34,18 +35,20 @@
 
 def kernel(
     dp_size,
-    offsets,
-    counts,
+    offsets_hbm,
+    counts_hbm,
     tok_hbm,
-    cot,
+    cot_hbm,
     old_master,
     old_moment,
     old_variance,
     old_grad,
     act_out,
-    master_out,
-    moment_out,
-    variance_out,
+    state_out,
+    offsets,
+    counts,
+    cot,
+    flat_old,
     tok,
     tok_t,
     old,
@@ -66,7 +69,7 @@
     minus_in,
     tile_out,
     tile_in,
-    tok_sem,
+    in_sems,
     edge_sems,
     ring_send,
     z_recv,
@@ -99,8 +102,6 @@
     core = lax.rem(dp, 2)
     z = lax.rem(lax.div(dp, 2), depth)
     y_lo = lax.div(dp, 2 * depth)
-    a = lax.div(z, STRIDE)
-    b = lax.rem(z, STRIDE)
 
     def device(dz=0, flip_lo=0, flip_group=0, flip_core=0):
         to_z = lax.rem(z + dz + depth, depth)
@@ -135,8 +136,16 @@
     def arrived(dst, recv_sem):
         remote(dst, dst, recv_sem, recv_sem, other_core).wait_recv()
 
-    tok_copy = pltpu.make_async_copy(tok_hbm, tok, tok_sem)
-    tok_copy.start()
+    olds = (old_master, old_moment, old_variance, old_grad)
+    copies = [pltpu.make_async_copy(ref.at[0], flat_old.at[i], in_sems.at[i]) for i, ref in enumerate(olds)]
+    copies.append(pltpu.make_async_copy(offsets_hbm, offsets, in_sems.at[4]))
+    late = [
+        pltpu.make_async_copy(tok_hbm, tok, in_sems.at[5]),
+        pltpu.make_async_copy(cot_hbm, cot, in_sems.at[6]),
+        pltpu.make_async_copy(counts_hbm, counts, in_sems.at[7]),
+    ]
+    for copy in copies + late:
+        copy.start()
 
     barrier = pltpu.get_barrier_semaphore()
     greeted = [right, left, other_core, *y_peers]
@@ -144,10 +153,12 @@
     for peer in greeted:
         pl.semaphore_signal(barrier, inc=1, device_id=peer, device_id_type=MESH)
 
+    for copy in copies:
+        copy.wait()
     for r in range(window_rows):
         lanes = slice(r * LANES, (r + 1) * LANES)
-        for i, ref in enumerate((old_master, old_moment, old_variance, old_grad)):
-            old[i, r : r + 1, :] = ref[0, :, lanes]
+        for i in range(4):
+            old[i, r : r + 1, :] = flat_old[i, :, lanes]
     updated = adam_update(old[0], old[1], old[2], old[3], first_step)
     shape = (window_rows, LANES)
     position = (
@@ -176,55 +187,71 @@
         state[i, rows - margin : rows, :] += edge_in[1, i]
 
     line = w.at[group, y_lo, core]
-    line[z] = state[0].astype(BF16)
-
-    def at(k):
-        return lax.rem(z + STRIDE * k + depth, depth)
-
-    def ring(slot, step, direction):
-        index = step if direction > 0 else half + step
-        send(line.at[slot], line.at[slot], ring_send.at[index], z_recv.at[slot], device(dz=direction * STRIDE))
-
-    def near(slot):
-        block = lax.div(slot, STRIDE)
-        far = 2 - 4 * lax.rem(block, 2)
-        for i, d in enumerate((1, -1, far)):
-            send(line.at[slot], line.at[slot], near_send.at[i, block], z_recv.at[slot], device(dz=d))
+    base = STRIDE * (half - 1) + 1
+
+    def ring(k, direction):
+        to = k - direction
+        to = half if to == -half else to
+        src, dst = base + STRIDE * k, base + STRIDE * to
+        index = -k if direction > 0 else half + k
+        send(line.at[src], line.at[dst], ring_send.at[index], z_recv.at[dst], device(dz=direction * STRIDE))
+
+    def near(k):
+        src = base + STRIDE * k
+        for i, d in enumerate((-1, 1, -2)):
+            send(line.at[src], line.at[src - d], near_send.at[i, k + half - 1], z_recv.at[src - d], device(dz=d))
 
     def along_y(k):
-        block = lax.rem(a + k + members, members)
-        for d in range(1, STRIDE):
-            slot = block * STRIDE + lax.rem(b + d, STRIDE)
+        block = k + half - 1
+        for d in (-1, 1, 2):
+            slot = base + STRIDE * k + d
             arrived(line.at[slot], z_recv.at[slot])
         piece = line.at[pl.ds(block * STRIDE, STRIDE)]
         for i, peer in enumerate(y_peers):
             send(piece, piece, y_send.at[i, block], y_recv.at[i, block], peer)
 
-    ring(z, 0, 1)
-    if half > 1:
-        ring(z, 0, -1)
-    near(z)
-
-    tok_copy.wait()
-    for i in range(tok.shape[1] // LANES):
-        lanes = slice(i * LANES, (i + 1) * LANES)
-        tok_t[lanes, :] = tok[:, lanes].T
-
-    for k in range(1, half + 1):
-        slot = at(-k)
+    def from_ring(k):
+        slot = base + STRIDE * k
         arrived(line.at[slot], z_recv.at[slot])
-        if k < half:
-            ring(slot, k, 1)
-        near(slot)
-        if k < half:
-            slot = at(k)
-            arrived(line.at[slot], z_recv.at[slot])
-            if k < half - 1:
-                ring(slot, k, -1)
-            near(slot)
+
+    line[base] = state[0].astype(BF16)
+    ring(0, 1)
+    ring(0, -1)
+    near(0)
+
+    for copy in late:
+        copy.wait()
+    low_slot = STRIDE * (half - 1) + 2
+    group_z = 8
+    group_rows = group_z * 2 * rows
+
+    def transpose(i, carry):
+        columns = tok[:, pl.ds(pl.multiple_of(i * group_rows, group_rows), group_rows)].T
+        for n in range(group_z):
+            nat = i * group_z + n
+            lo = lax.div(nat, depth)
+            slot = lax.rem(lax.rem(nat, depth) - z + low_slot + depth, depth)
+            start = pl.multiple_of((lo * depth + slot) * (2 * rows), 2 * rows)
+            tok_t[pl.ds(start, 2 * rows), :] = columns[n * 2 * rows : (n + 1) * 2 * rows, :]
+        return carry
+
+    lax.fori_loop(0, 2 * depth // group_z, transpose, 0)
+
+    for k in range(1, half):
+        from_ring(-k)
+        ring(-k, 1)
+        near(-k)
+        from_ring(k)
+        if k < half - 1:
+            ring(k, -1)
+        near(k)
         along_y(1 - k)
         if k > 1:
             along_y(k - 1)
+    from_ring(half)
+    near(half)
+    along_y(1 - half)
+    along_y(half - 1)
     along_y(half)
 
     def to_core(i, lo, g):
@@ -248,7 +275,8 @@
 
     def flatten(zz, carry):
         for lo in range(2):
-            start = pl.multiple_of((lo * depth + zz) * (2 * rows), 2 * rows)
+            to_z = lax.rem(z + zz - base + depth, depth)
+            start = pl.multiple_of((lo * depth + to_z) * (2 * rows), 2 * rows)
             for g in range(2):
                 both = jnp.concatenate([w[g, lo, 0, zz], w[g, lo, 1, zz]], axis=0)
                 w_flat[pl.ds(start, 2 * rows), g * LANES : (g + 1) * LANES] = both
@@ -264,11 +292,11 @@
     delta = jnp.where(row_live, cot[...].astype(F32) * derivative, F32(0.0)).astype(BF16)
 
     order = [half] + [s * k for k in range(half - 1, 0, -1) for s in (1, -1)] + [0]
-    blocks = [lax.rem(a + k + members, members) for k in order]
+    blocks = [k + half - 1 for k in order]
     for block in blocks:
         for lo in range(2):
             count = STRIDE * 2 * rows
-            start = pl.multiple_of((lo * depth + block * STRIDE) * (2 * rows), count)
+            start = (lo * depth + block * STRIDE) * (2 * rows)
             part = jnp.dot(tok_t[pl.ds(start, count), :], delta, preferred_element_type=F32)
             for zz in range(STRIDE):
                 for c in range(2):
@@ -276,7 +304,8 @@
                     for g in range(2):
                         parts[c, block, g, lo, zz] = part[top : top + rows, g * LANES : (g + 1) * LANES].astype(BF16)
         send(parts.at[1 - core, block], core_in.at[block], part_send.at[block], part_recv.at[block], other_core)
-    for block in blocks:
+    def over_core(j):
+        block = blocks[j]
         arrived(core_in.at[block], part_recv.at[block])
         both = parts[core, block].astype(F32) + core_in[block].astype(F32)
         parts[core, block] = both.astype(BF16)
@@ -292,14 +321,13 @@
             arrived(y_in.at[i, block], sum_recv.at[i, block])
             total += y_in[i, block].astype(F32)
         z_sum[block] = total.astype(BF16)
-        far = 2 - 4 * lax.rem(block, 2)
-        for i, (d, dz) in enumerate(((1, 1), (3, -1), (2, far))):
-            src = z_sum.at[block, lax.rem(b + d, STRIDE)]
+        for i, dz in enumerate((-2, -1, 1)):
+            src = z_sum.at[block, 2 + dz]
             send(src, near_in.at[i, block], window_send.at[i, block], window_recv.at[i, block], device(dz=dz))
 
     def over_ring(j):
         block, k = blocks[j], order[j]
-        total = z_sum[block, b].astype(F32)
+        total = z_sum[block, 2].astype(F32)
         for i in range(3):
             arrived(near_in.at[i, block], window_recv.at[i, block])
             total += near_in[i, block].astype(F32)
@@ -321,9 +349,13 @@
             send(minus_out.at[s], minus_in.at[s], minus_sems.at[0, s], minus_sems.at[1, s], device(dz=-STRIDE))
         return total
 
+    for j in range(IN_FLIGHT):
+        over_core(j)
     for j in range(members + 1):
         if j < members:
             over_y(j)
+        if j + IN_FLIGHT < members:
+            over_core(j + IN_FLIGHT)
         if j >= 1:
             gradient = over_ring(j - 1)
 
@@ -335,13 +367,19 @@
         tile_out[i] = jnp.where(first, bottom, top)
     send(tile_out, tile_in, tile_sems.at[0], tile_sems.at[1], y_peers[2])
     arrived(tile_in, tile_sems.at[1])
-    for i, ref in enumerate((master_out, moment_out, variance_out)):
+    for i in range(3):
         top, bottom = state[i, 0:tile, :], state[i, tile:rows, :]
         kept = jnp.where(first, top, bottom)
-        ref[:, 0:LANES] = jnp.where(first, kept, tile_in[i])
-        ref[:, LANES : 2 * LANES] = jnp.where(first, tile_in[i], kept)
+        state_out[i, :, 0:LANES] = jnp.where(first, kept, tile_in[i])
+        state_out[i, :, LANES : 2 * LANES] = jnp.where(first, tile_in[i], kept)
     for copy in pending:
         copy.wait_send()
+
+
+def finish(act, state, act_out, master_out, moment_out, variance_out):
+    act_out[...] = act[...]
+    for i, ref in enumerate((master_out, moment_out, variance_out)):
+        ref[...] = state[i]
 
 
 def solution(mesh):
@@ -359,14 +397,18 @@
         out = jax.ShapeDtypeStruct((tile, 2 * LANES), F32)
         piece = (rows, LANES)
         vmem = pl.BlockSpec(memory_space=pltpu.VMEM)
-        smem = pl.BlockSpec(memory_space=pltpu.SMEM)
         dma = pltpu.SemaphoreType.DMA
-        return pl.pallas_call(
+        act_shape = jax.ShapeDtypeStruct(cotangent.shape, BF16)
+        act, new_state = pl.pallas_call(
             functools.partial(kernel, dp_size),
-            out_shape=(jax.ShapeDtypeStruct(cotangent.shape, BF16), out, out, out),
-            in_specs=[smem, smem, pl.BlockSpec(memory_space=pl.ANY)] + [vmem] * 5,
-            out_specs=(vmem,) * 4,
+            out_shape=(act_shape, jax.ShapeDtypeStruct((3, tile, 2 * LANES), F32)),
+            in_specs=[pl.BlockSpec(memory_space=pltpu.HBM)] * 8,
+            out_specs=(vmem,) * 2,
             scratch_shapes=[
+                pltpu.SMEM(old_offsets.shape, jnp.int32),
+                pltpu.SMEM(counts.shape, jnp.int32),
+                pltpu.VMEM(cotangent.shape, BF16),
+                pltpu.VMEM((4, 1, old_master.shape[-1]), F32),
                 pltpu.VMEM((token_rows, width), BF16),
                 pltpu.VMEM((width, token_rows), BF16),
                 pltpu.VMEM((4, window_rows, LANES), F32),
@@ -387,7 +429,7 @@
                 pltpu.VMEM((half, *piece), BF16),
                 pltpu.VMEM((3, tile, LANES), F32),
                 pltpu.VMEM((3, tile, LANES), F32),
-                dma(()),
+                dma((8,)),
                 dma((4,)),
                 dma((2 * half,)),
                 dma((depth,)),
@@ -406,8 +448,16 @@
                 dma((2, half)),
                 dma((2,)),
             ],
-            compiler_params=pltpu.CompilerParams(collective_id=0, has_side_effects=True),
+            compiler_params=pltpu.CompilerParams(
+                collective_id=0, has_side_effects=True, vmem_limit_bytes=60 * 1024 * 1024
+            ),
         )(old_offsets, counts, tokens, cotangent, old_master, old_moment, old_variance, old_grad)
+        return pl.pallas_call(
+            finish,
+            out_shape=(act_shape, out, out, out),
+            in_specs=[vmem] * 2,
+            out_specs=(vmem,) * 4,
+        )(act, new_state)
 
     state_spec = P(("tensor", "group"), "dp", None)
     row_spec = P(("dp", "group"), "tensor")

time: 117 us -> 91.4 us (0.78)
  Pallas kernels: 111 us -> 90.6 us
  local copies, waits for them, and re-layouts: 5.51 us -> 0 us
    pallas_call x1 -> x2, Pallas kernels: 111 us -> 90.6 us  [the longest x1 89 us: local(): pl.pallas_call(functools.partial(kernel, dp_size), out_shape=(act_shape,...]
    unnamed x4 -> x0, local copies, waits for them, and re-layouts: 5.51 us -> none
where the time goes in v2:
time: 91.4 us; the launch traced here: 91.2 us
  Pallas kernels  90.6 us (99%)
    pallas_call x1, Pallas kernels, local(): pl.pallas_call(functools.partial(kernel, dp_size), out_shape=(act_shape,...  89 us

profile of v2, /device:TPU:6, one launch (start us, length us, event | category | flops | bytes accessed | tf_op | source)
XLA Modules:
  0.0 91.2 jit_solution(17467940206574628256)
XLA Ops:
  0.6 89.0 %shard_map.111 = (bf16[128,256]{1,0:T(8,128)(2,1)}, f32[3,20,256]{2,1,0:T(8,128)}) custom-call(s32[8,129]{1,0:T(8,128)} %offsets_hbm.1, s32[256]{0:T(256)} %counts_hbm.1, bf16[128,5120]{1,0:T(8,128)(2,1)} %tok_hbm.1, bf16[128,256]{1,0:T(8,128)(2,1)} %cot_hbm.1, f32[1,1,6400]{2,1,0:T(1,128)} %old_master.1, f32[1,1,6400]{2,1,0:T(1,128)} %old_moment.1, ...), custom_call_target="tpu_custom_call" | custom-call | tf_op jit(solution)/shard_map/pallas_call | solution.py:402
  89.6 1.6 %shard_map.112 = (bf16[128,256]{1,0:T(8,128)(2,1)}, f32[20,256]{1,0:T(8,128)}, f32[20,256]{1,0:T(8,128)}, f32[20,256]{1,0:T(8,128)}) custom-call(bf16[128,256]{1,0:T(8,128)(2,1)} %get-tuple-element.6.act, f32[3,20,256]{2,1,0:T(8,128)} %get-tuple-element.7.state), custom_call_target="tpu_custom_call" | custom-call | tf_op jit(solution)/shard_map/pallas_call | solution.py:455

commit v3 on v2

--- a/solution.py
+++ b/solution.py
@@ -69,6 +69,11 @@
     minus_in,
     tile_out,
     tile_in,
+    kept,
+    ends,
+    ends_out,
+    ends_in,
+    act,
     in_sems,
     edge_sems,
     ring_send,
@@ -87,6 +92,8 @@
     plus_sems,
     minus_sems,
     tile_sems,
+    end_sems,
+    act_sem,
 ):
     depth = dp_size // 4
     members = depth // STRIDE
@@ -150,6 +157,7 @@
     barrier = pltpu.get_barrier_semaphore()
     greeted = [right, left, other_core, *y_peers]
     greeted += [device(dz=d) for d in (STRIDE, -STRIDE, 1, -1, 2, -2)]
+    greeted += [device(dz=d, flip_group=1) for d in (STRIDE, -STRIDE)]
     for peer in greeted:
         pl.semaphore_signal(barrier, inc=1, device_id=peer, device_id_type=MESH)
 
@@ -186,6 +194,12 @@
         state[i, 0:margin, :] += edge_in[0, i]
         state[i, rows - margin : rows, :] += edge_in[1, i]
 
+    first = group == 0
+    for i in range(3):
+        top, bottom = state[i, 0:tile, :], state[i, tile:rows, :]
+        tile_out[i] = jnp.where(first, bottom, top)
+        kept[i] = jnp.where(first, top, bottom)
+
     line = w.at[group, y_lo, core]
     base = STRIDE * (half - 1) + 1
 
@@ -218,6 +232,9 @@
     ring(0, 1)
     ring(0, -1)
     near(0)
+
+    partner = y_peers[2]
+    send(tile_out, tile_in, tile_sems.at[0], tile_sems.at[1], partner)
 
     for copy in late:
         copy.wait()
@@ -285,7 +302,9 @@
     lax.fori_loop(0, depth, flatten, 0)
     preact = jnp.dot(tok[...], w_flat[...], preferred_element_type=F32)
     sigmoid_z = jax.nn.sigmoid(preact)
-    act_out[...] = (preact * sigmoid_z).astype(BF16)
+    act[...] = (preact * sigmoid_z).astype(BF16)
+    act_copy = pltpu.make_async_copy(act, act_out, act_sem)
+    act_copy.start()
     derivative = sigmoid_z * (1.0 + preact * (1.0 - sigmoid_z))
     my_count = counts[dp * 2 + group]
     row_live = lax.broadcasted_iota(jnp.int32, preact.shape, 0) < my_count
@@ -325,12 +344,31 @@
             src = z_sum.at[block, 2 + dz]
             send(src, near_in.at[i, block], window_send.at[i, block], window_recv.at[i, block], device(dz=dz))
 
+    def halves(i, total, dz):
+        ends[i, 0] = total[0:tile]
+        ends[i, 1] = total[tile:rows]
+        ends_out[i] = ends[i].astype(BF16)
+        for own, to in ((1, device(dz=dz)), (0, device(dz=dz, flip_group=1))):
+            if own and dz == 0:
+                continue
+            half_rows = group if own else 1 - group
+            n = 4 if dz == 0 else 2 * i + 1 - own
+            send(ends_out.at[i, half_rows], ends_in.at[n], end_sems.at[0, n], end_sems.at[1, n], to)
+
     def over_ring(j):
         block, k = blocks[j], order[j]
         total = z_sum[block, 2].astype(F32)
         for i in range(3):
             arrived(near_in.at[i, block], window_recv.at[i, block])
             total += near_in[i, block].astype(F32)
+        if k == 0:
+            halves(2, total, 0)
+            own_sum = jnp.where(first, total[0:tile], total[tile:rows])
+            for n in range(5):
+                arrived(ends_in.at[n], end_sems.at[1, n])
+            mine = own_sum + ends_in[0].astype(F32) + ends_in[2].astype(F32)
+            theirs = ends_in[1].astype(F32) + ends_in[3].astype(F32) + ends_in[4].astype(F32)
+            return mine, theirs
         if k >= 0 and k < half:
             s = half - 1 - k
             arrived(plus_in.at[s], plus_sems.at[1, s])
@@ -339,11 +377,13 @@
             s = half - 2 + k
             arrived(minus_in.at[s], minus_sems.at[1, s])
             total += minus_in[s].astype(F32)
-        if k > 0:
+        if k == 1 or k == -1:
+            halves(0 if k > 0 else 1, total, STRIDE * k)
+        elif k > 0:
             s = half - k
             plus_out[s] = total.astype(BF16)
             send(plus_out.at[s], plus_in.at[s], plus_sems.at[0, s], plus_sems.at[1, s], device(dz=STRIDE))
-        if k < 0:
+        elif k < 0:
             s = half - 1 + k
             minus_out[s] = total.astype(BF16)
             send(minus_out.at[s], minus_in.at[s], minus_sems.at[0, s], minus_sems.at[1, s], device(dz=-STRIDE))
@@ -359,19 +399,13 @@
         if j >= 1:
             gradient = over_ring(j - 1)
 
-    new = adam_update(state[0], state[1], state[2], gradient, second_step)
-    first = group == 0
-    for i in range(3):
-        state[i] = new[i]
-        top, bottom = state[i, 0:tile, :], state[i, tile:rows, :]
-        tile_out[i] = jnp.where(first, bottom, top)
-    send(tile_out, tile_in, tile_sems.at[0], tile_sems.at[1], y_peers[2])
     arrived(tile_in, tile_sems.at[1])
-    for i in range(3):
-        top, bottom = state[i, 0:tile, :], state[i, tile:rows, :]
-        kept = jnp.where(first, top, bottom)
-        state_out[i, :, 0:LANES] = jnp.where(first, kept, tile_in[i])
-        state_out[i, :, LANES : 2 * LANES] = jnp.where(first, tile_in[i], kept)
+    for lanes, old_state, summed in ((group, kept, gradient[0]), (1 - group, tile_in, gradient[1])):
+        new = adam_update(old_state[0], old_state[1], old_state[2], summed, second_step)
+        start = pl.multiple_of(lanes * LANES, LANES)
+        for i in range(3):
+            state_out[i, :, pl.ds(start, LANES)] = new[i]
+    act_copy.wait()
     for copy in pending:
         copy.wait_send()
 
@@ -403,7 +437,7 @@
             functools.partial(kernel, dp_size),
             out_shape=(act_shape, jax.ShapeDtypeStruct((3, tile, 2 * LANES), F32)),
             in_specs=[pl.BlockSpec(memory_space=pltpu.HBM)] * 8,
-            out_specs=(vmem,) * 2,
+            out_specs=(pl.BlockSpec(memory_space=pltpu.HBM), vmem),
             scratch_shapes=[
                 pltpu.SMEM(old_offsets.shape, jnp.int32),
                 pltpu.SMEM(counts.shape, jnp.int32),
@@ -429,6 +463,11 @@
                 pltpu.VMEM((half, *piece), BF16),
                 pltpu.VMEM((3, tile, LANES), F32),
                 pltpu.VMEM((3, tile, LANES), F32),
+                pltpu.VMEM((3, tile, LANES), F32),
+                pltpu.VMEM((3, 2, tile, LANES), F32),
+                pltpu.VMEM((3, 2, tile, LANES), BF16),
+                pltpu.VMEM((5, tile, LANES), BF16),
+                pltpu.VMEM(cotangent.shape, BF16),
                 dma((8,)),
                 dma((4,)),
                 dma((2 * half,)),
@@ -447,6 +486,8 @@
                 dma((2, half)),
                 dma((2, half)),
                 dma((2,)),
+                dma((2, 5)),
+                dma(()),
             ],
             compiler_params=pltpu.CompilerParams(
                 collective_id=0, has_side_effects=True, vmem_limit_bytes=60 * 1024 * 1024

time: 91.4 us -> 90.2 us (0.987)
  Pallas kernels: 90.6 us -> 89.3 us
    pallas_call x1, Pallas kernels: 89 us -> 87.7 us  [local(): pl.pallas_call(functools.partial(kernel, dp_size), out_shape=(act_shape,...]
where the time goes in v3:
time: 90.2 us; the launch traced here: 89.9 us
  Pallas kernels  89.3 us (99%)
    pallas_call x1, Pallas kernels, local(): pl.pallas_call(functools.partial(kernel, dp_size), out_shape=(act_shape,...  87.7 us

profile of v3, /device:TPU:6, one launch (start us, length us, event | category | flops | bytes accessed | tf_op | source)
XLA Modules:
  0.0 89.9 jit_solution(8466841672061321057)
XLA Ops:
  0.6 87.7 %shard_map.111 = (bf16[128,256]{1,0:T(8,128)(2,1)}, f32[3,20,256]{2,1,0:T(8,128)}) custom-call(s32[8,129]{1,0:T(8,128)} %offsets_hbm.1, s32[256]{0:T(256)} %counts_hbm.1, bf16[128,5120]{1,0:T(8,128)(2,1)} %tok_hbm.1, bf16[128,256]{1,0:T(8,128)(2,1)} %cot_hbm.1, f32[1,1,6400]{2,1,0:T(1,128)} %old_master.1, f32[1,1,6400]{2,1,0:T(1,128)} %old_moment.1, ...), custom_call_target="tpu_custom_call" | custom-call | tf_op jit(solution)/shard_map/pallas_call | solution.py:436
  88.4 1.6 %shard_map.112 = (bf16[128,256]{1,0:T(8,128)(2,1)}, f32[20,256]{1,0:T(8,128)}, f32[20,256]{1,0:T(8,128)}, f32[20,256]{1,0:T(8,128)}) custom-call(bf16[128,256]{1,0:T(8,128)(2,1)} %get-tuple-element.6.act, f32[3,20,256]{2,1,0:T(8,128)} %get-tuple-element.7.state), custom_call_target="tpu_custom_call" | custom-call | tf_op jit(solution)/shard_map/pallas_call | solution.py:496

commit v4 on v3

--- a/solution.py
+++ b/solution.py
@@ -20,7 +20,7 @@
 second_step = 4.0
 
 LANES = 128
-IN_FLIGHT = 2
+IN_FLIGHT = 3
 STRIDE = 4
 
 
@@ -143,6 +143,13 @@
     def arrived(dst, recv_sem):
         remote(dst, dst, recv_sem, recv_sem, other_core).wait_recv()
 
+    barrier = pltpu.get_barrier_semaphore()
+    greeted = [right, left, other_core, *y_peers]
+    greeted += [device(dz=d) for d in (STRIDE, -STRIDE, 1, -1, 2, -2)]
+    greeted += [device(dz=d, flip_group=1) for d in (STRIDE, -STRIDE)]
+    for peer in greeted:
+        pl.semaphore_signal(barrier, inc=1, device_id=peer, device_id_type=MESH)
+
     olds = (old_master, old_moment, old_variance, old_grad)
     copies = [pltpu.make_async_copy(ref.at[0], flat_old.at[i], in_sems.at[i]) for i, ref in enumerate(olds)]
     copies.append(pltpu.make_async_copy(offsets_hbm, offsets, in_sems.at[4]))
@@ -153,13 +160,6 @@
     ]
     for copy in copies + late:
         copy.start()
-
-    barrier = pltpu.get_barrier_semaphore()
-    greeted = [right, left, other_core, *y_peers]
-    greeted += [device(dz=d) for d in (STRIDE, -STRIDE, 1, -1, 2, -2)]
-    greeted += [device(dz=d, flip_group=1) for d in (STRIDE, -STRIDE)]
-    for peer in greeted:
-        pl.semaphore_signal(barrier, inc=1, device_id=peer, device_id_type=MESH)
 
     for copy in copies:
         copy.wait()
@@ -252,7 +252,9 @@
             tok_t[pl.ds(start, 2 * rows), :] = columns[n * 2 * rows : (n + 1) * 2 * rows, :]
         return carry
 
-    lax.fori_loop(0, 2 * depth // group_z, transpose, 0)
+    steps = 2 * depth // group_z
+    per_ring_step = steps // half
+    lax.fori_loop(0, per_ring_step, transpose, 0)
 
     for k in range(1, half):
         from_ring(-k)
@@ -262,6 +264,7 @@
         if k < half - 1:
             ring(k, -1)
         near(k)
+        lax.fori_loop(k * per_ring_step, (k + 1) * per_ring_step, transpose, 0)
         along_y(1 - k)
         if k > 1:
             along_y(k - 1)

time: 90.2 us -> 90.1 us (level)
  no operation moved by 1% of the time
where the time goes in v4:
time: 90.1 us; the launch traced here: 89.8 us
  Pallas kernels  89.1 us (99%)
    pallas_call x1, Pallas kernels, local(): pl.pallas_call(functools.partial(kernel, dp_size), out_shape=(act_shape,...  87.6 us

profile of v4, /device:TPU:6, one launch (start us, length us, event | category | flops | bytes accessed | tf_op | source)
XLA Modules:
  0.0 89.8 jit_solution(492661250469660686)
XLA Ops:
  0.6 87.6 %shard_map.111 = (bf16[128,256]{1,0:T(8,128)(2,1)}, f32[3,20,256]{2,1,0:T(8,128)}) custom-call(s32[8,129]{1,0:T(8,128)} %offsets_hbm.1, s32[256]{0:T(256)} %counts_hbm.1, bf16[128,5120]{1,0:T(8,128)(2,1)} %tok_hbm.1, bf16[128,256]{1,0:T(8,128)(2,1)} %cot_hbm.1, f32[1,1,6400]{2,1,0:T(1,128)} %old_master.1, f32[1,1,6400]{2,1,0:T(1,128)} %old_moment.1, ...), custom_call_target="tpu_custom_call" | custom-call | tf_op jit(solution)/shard_map/pallas_call | solution.py:439
  88.2 1.6 %shard_map.112 = (bf16[128,256]{1,0:T(8,128)(2,1)}, f32[20,256]{1,0:T(8,128)}, f32[20,256]{1,0:T(8,128)}, f32[20,256]{1,0:T(8,128)}) custom-call(bf16[128,256]{1,0:T(8,128)(2,1)} %get-tuple-element.6.act, f32[3,20,256]{2,1,0:T(8,128)} %get-tuple-element.7.state), custom_call_target="tpu_custom_call" | custom-call | tf_op jit(solution)/shard_map/pallas_call | solution.py:499
